TPU v7x, 32 devices: a whole 2x2x4 slice. The times are simulated.
32 devices in a mesh: row: 8 (over y, x, core), col: 4 (over z).
Axes of the slice: x: 2, y: 2, z: 4, core: 2. Of those that a mesh axis runs over, the one named last changes fastest.
Arguments:
- panel_tiles: float32 [16384, 1024], P('row', 'col'), may hold values from -48 to 48
- left_u: bfloat16 [16384, 6144], P('row', 'col'), may hold values from -8 to 8
- earlier_right_factors: bfloat16 [16384, 6144], P('row', 'col'), may hold values from -0.25 to 0.25
- tile_global_index: int32 [16], replicated, may hold values from 0 to 15, as said below
Outputs:
- panel_factor: float32 [16384, 1024], P('row', 'col')
Inputs may be any that keep to these rules, and one draw needn't show every extreme that they name: `tile_global_index`: A permutation; slot pivot, the one numbered 0, holds the diagonal tile.
All inputs are finite; a program needn't handle non-finite values.
Results may differ from a plain program's by a relative error of at most 0.00053.
Values may be sent and summed in bfloat16 or wider, within the bound.
A program may use at most 128 MiB of HBM per device.

v0:
```python
import functools

import jax
import jax.numpy as jnp
from jax import lax
from jax.experimental import pallas as pl
from jax.experimental.pallas import tpu as pltpu
from jax.sharding import PartitionSpec as P

TILE = 1024
RANK = 256

BLK = 128
SUB = 8
FILL = 256
STRIP = 256
GROUP = 256
SKEW = 3
LAG = 2
F32 = jnp.float32
BF16 = jnp.bfloat16
HI = lax.Precision.HIGHEST
MESH = pl.DeviceIdType.MESH
ANY = pl.BlockSpec(memory_space=pl.ANY)
VM = pl.BlockSpec(memory_space=pltpu.VMEM)
TRANS = (((1,), (1,)), ((), ()))


def dot(a, b, dims=((1,), (0,))):
    return lax.dot_general(a, b, (dims, ((), ())), precision=HI, preferred_element_type=F32)


def window(start, size):
    return pl.ds(pl.multiple_of(start, size), size)


def remote(src, dst, send, recv, target):
    return pltpu.make_async_remote_copy(
        src_ref=src, dst_ref=dst, send_sem=send, recv_sem=recv, device_id=target, device_id_type=MESH
    )


def pick(table, index):
    value = jnp.int32(table[0])
    for i in range(1, len(table)):
        value = jnp.where(index == i, jnp.int32(table[i]), value)
    return value


def spread_kernel(
    owner, row_devices, pieces, mask_ref, v_ref, u_ref, a_ref, left_ref, pu_ref, part_ref,
    pv, v_own, u_own, a_own, pvt, pin, left_own, small, a_mine, a_got, sends, recvs, a_send, a_recv, local_sem,
):
    me = lax.axis_index("row")
    col = lax.axis_index("col")
    chips = row_devices // 2
    chip, core = me // 2, me % 2
    order = [i ^ (i >> 1) for i in range(chips)]
    if max(order) >= chips:
        order = list(range(chips))
    home = order.index(owner // 2)
    home_core = owner % 2
    place = pick([order.index(c) for c in range(chips)], chip)
    nexts = [pick(order, (place + chips + w) % chips) * 2 + core for w in (1, -1)]
    hops = [(chips + w * (place - home)) % chips for w in (1, -1)]
    pair = chip * 2 + 1 - core
    tile, width = pu_ref.shape
    half = tile // 2
    step = half // (2 * pieces)
    share = tile // row_devices
    rank = RANK
    blocks = width // rank
    slots = v_ref.shape[0] // tile

    loads = [
        pltpu.make_async_copy(src, dst, local_sem.at[i])
        for i, (src, dst) in enumerate(((v_ref, v_own), (u_ref, u_own), (a_ref, a_own)))
    ]
    loads[0].start()

    barrier = pltpu.get_barrier_semaphore()
    for d in range(1, row_devices):
        pl.semaphore_signal(barrier, inc=1, device_id=((me + d) % row_devices, col), device_id_type=MESH)
    pl.semaphore_wait(barrier, row_devices - 1)
    loads[0].wait()
    loads[1].start()
    loads[2].start()

    bufs = (pv, pu_ref)

    def move(kind, way, side, i, target, lane):
        at = window(way * half + (2 * i + side) * step, step)
        ref = bufs[kind].at[at, :]
        return remote(ref, ref, sends.at[kind, lane, way, i], recvs.at[kind, way, side, i], (target, col))

    is_owner = me == owner
    away = chip != owner // 2
    helper = jnp.logical_and(jnp.logical_not(away), jnp.logical_not(is_owner))

    def a_piece(target):
        return remote(a_mine.at[window(target * share, share), :], a_got, a_send.at[target], a_recv, (target, col))

    def chosen(src, dst):
        @pl.loop(0, tile // BLK)
        def _(n):
            total = None
            for t in range(slots):
                keep = mask_ref[t:t + 1, :dst.shape[1]].astype(dst.dtype)
                term = src[window(t * tile + n * BLK, BLK), :] * keep
                total = term if total is None else total + term
            dst[window(n * BLK, BLK), :] = total

    def first_sends(kind):
        @pl.loop(0, pieces)
        def _(i):
            for way in range(2):
                move(kind, way, 1 - home_core, i, owner ^ 1, 2).start()
                move(kind, way, home_core, i, nexts[way], 0).start()
            for way in range(2):
                move(kind, way, home_core, i, owner ^ 1, 1).start()

    @pl.when(is_owner)
    def _():
        chosen(v_own, pv)
        first_sends(0)
        loads[1].wait()
        chosen(u_own, pu_ref)
        first_sends(1)
        loads[2].wait()
        chosen(a_own, a_mine)
        for other in range(row_devices):
            if other != owner:
                a_piece(other).start()
        a_got[...] = a_mine[owner * share:(owner + 1) * share, :]

    @pl.when(jnp.logical_not(is_owner))
    def _():
        loads[1].wait()
        loads[2].wait()

    def relay(kind, tick):
        for way in range(2):
            i = tick - SKEW * jnp.maximum(hops[way] - 1, 0)

            @pl.when(jnp.logical_and(jnp.logical_not(is_owner), jnp.logical_and(i >= 0, i < pieces)))
            def _():
                move(kind, way, core, i, nexts[way], 0).wait_recv()

                @pl.when(hops[way] < chips - 1)
                def _():
                    move(kind, way, core, i, nexts[way], 0).start()

                @pl.when(away)
                def _():
                    move(kind, way, core, i, pair, 1).start()

    def gather(kind):
        @pl.when(jnp.logical_not(is_owner))
        def _():
            @pl.loop(0, pieces)
            def _(i):
                for way in range(2):
                    move(kind, way, 1 - core, i, pair, 1).wait_recv()

    ticks = pieces + SKEW * max(chips - 2, 0)

    @pl.loop(0, ticks)
    def _(tick):
        relay(0, tick)

    gather(0)
    each = max(1, ticks // (blocks * slots))
    during = min(ticks, each * blocks * slots)

    @pl.loop(0, blocks)
    def _(b):
        at = window(b * rank, rank)
        pvt[at, :] = pv[:, at].T
        pin[:, at] = jnp.dot(pvt[at, :], pv[:, at], preferred_element_type=F32).astype(BF16)

        @pl.loop(0, slots)
        def _(t):
            here = window(t * tile, tile)
            inner = jnp.dot(pvt[at, :], v_own[here, at], preferred_element_type=F32).astype(BF16)
            left_own[here, at] = lax.dot_general(
                u_own[here, at], inner, TRANS, preferred_element_type=F32
            ).astype(BF16)
            done = (b * slots + t) * each

            @pl.loop(jnp.minimum(done, during), jnp.minimum(done + each, during))
            def _(tick):
                relay(1, tick)

    left_out = pltpu.make_async_copy(left_own, left_ref, local_sem.at[3])
    left_out.start()

    @pl.loop(during, ticks)
    def _(tick):
        relay(1, tick)

    gather(1)
    rows = window(me * share, share)

    @pl.loop(0, blocks)
    def _(b):
        at = window(b * rank, rank)
        small[:, at] = lax.dot_general(
            pu_ref[rows, at], pin[:, at], TRANS, preferred_element_type=F32
        ).astype(BF16)

    @pl.loop(0, tile // rank)
    def _(n):
        at = window(n * rank, rank)
        part_ref[:, at] = -lax.dot_general(small[...], pu_ref[at, :], TRANS, preferred_element_type=F32)

    @pl.when(jnp.logical_not(is_owner))
    def _():
        a_piece(owner).wait_recv()

    mine_cols = window(col * a_got.shape[1], a_got.shape[1])
    part_ref[:, mine_cols] = part_ref[:, mine_cols] + a_got[...]
    left_out.wait()

    @pl.when(is_owner)
    def _():
        for kind in range(2):

            @pl.loop(0, pieces)
            def _(i):
                for way in range(2):
                    move(kind, way, home_core, i, nexts[way], 0).wait_send()
                    move(kind, way, home_core, i, owner ^ 1, 1).wait_send()
                    move(kind, way, 1 - home_core, i, owner ^ 1, 2).wait_send()

        for other in range(row_devices):
            if other != owner:
                a_piece(other).wait_send()

    @pl.when(jnp.logical_not(is_owner))
    def _():
        for kind in range(2):

            @pl.loop(0, pieces)
            def _(i):
                for way in range(2):

                    @pl.when(hops[way] < chips - 1)
                    def _():
                        move(kind, way, core, i, nexts[way], 0).wait_send()

                    @pl.when(away)
                    def _():
                        move(kind, way, core, i, pair, 1).wait_send()


def spread(mesh, owner, mask, v, u, tiles):
    row_devices = mesh.shape["row"]
    tile, width = TILE, v.shape[1]
    pieces = 8
    share = tile // row_devices
    return pl.pallas_call(
        functools.partial(spread_kernel, owner, row_devices, pieces),
        out_shape=(
            jax.ShapeDtypeStruct(u.shape, BF16),
            jax.ShapeDtypeStruct((tile, width), BF16),
            jax.ShapeDtypeStruct((share, tile), F32),
        ),
        in_specs=[VM, ANY, ANY, ANY],
        out_specs=(ANY, VM, VM),
        scratch_shapes=[
            pltpu.VMEM((tile, width), BF16),
            pltpu.VMEM(v.shape, BF16),
            pltpu.VMEM(u.shape, BF16),
            pltpu.VMEM(tiles.shape, F32),
            pltpu.VMEM((width, tile), BF16),
            pltpu.VMEM((RANK, width), BF16),
            pltpu.VMEM(u.shape, BF16),
            pltpu.VMEM((share, width), BF16),
            pltpu.VMEM((tile, tiles.shape[1]), F32),
            pltpu.VMEM((share, tiles.shape[1]), F32),
            pltpu.SemaphoreType.DMA((2, 3, 2, pieces)),
            pltpu.SemaphoreType.DMA((2, 2, 2, pieces)),
            pltpu.SemaphoreType.DMA((row_devices,)),
            pltpu.SemaphoreType.DMA,
            pltpu.SemaphoreType.DMA((4,)),
        ],
        compiler_params=pltpu.CompilerParams(
            collective_id=1 + owner, has_side_effects=True, vmem_limit_bytes=48 * 1024 * 1024
        ),
        cost_estimate=pl.CostEstimate(flops=20_000_000_000, bytes_accessed=30_000_000, transcendentals=0),
        name="spread",
    )(mask, v, u, tiles)


def eliminate(block):
    shape = (SUB, BLK)
    groups = [block[g * SUB:(g + 1) * SUB, :] for g in range(BLK // SUB)]
    lane = lax.broadcasted_iota(jnp.int32, shape, 1)
    sub = lax.broadcasted_iota(jnp.int32, shape, 0)
    for g in range(len(groups)):
        base = g * SUB
        rows = groups[g]
        cols = [jnp.broadcast_to(rows[:, base + j:base + j + 1], shape) for j in range(SUB)]
        out = rows
        for s in range(SUB):
            raw = jnp.broadcast_to(rows[s:s + 1, :], shape)
            here = lane == base + s
            mine = sub == s
            out = jnp.where(mine, raw, out)
            inverse = 1.0 / jnp.broadcast_to(cols[s][s:s + 1, :], shape)
            factor = jnp.where(mine, 0.0, cols[s] * inverse)
            unit = jnp.where(here, 1.0, raw)
            kept = jnp.where(here, 0.0, rows)
            rows = jnp.where(mine, unit * inverse, kept - factor * unit)
            for j in range(s + 1, SUB):
                head = jnp.broadcast_to(cols[j][s:s + 1, :], shape)
                cols[j] = jnp.where(mine, head * inverse, cols[j] - factor * head)
        groups[g] = out
        if g + 1 == len(groups):
            break
        reduced = [jnp.broadcast_to(rows[s:s + 1, :], shape) for s in range(SUB)]
        inside = jnp.logical_and(lane >= base, lane < base + SUB)
        for h in range(g + 1, len(groups)):
            old = groups[h]
            terms = [
                jnp.broadcast_to(old[:, base + s:base + s + 1], shape) * reduced[s] for s in range(SUB)
            ]
            while len(terms) > 1:
                terms = [terms[i] + terms[i + 1] for i in range(0, len(terms), 2)]
            groups[h] = jnp.where(inside, 0.0, old) - terms[0]
    return jnp.concatenate(groups, axis=0)


def factor_step(k, w_ref, l_ref, x_ref):
    size = w_ref.shape[0]
    count = size // BLK
    row_id = lax.broadcasted_iota(jnp.int32, (BLK, BLK), 0)
    col_id = lax.broadcasted_iota(jnp.int32, (BLK, BLK), 1)
    at = window(k * BLK, BLK)
    done = eliminate(w_ref[at, at])
    pivots = jnp.sum(jnp.where(row_id == col_id, done, 0.0), axis=1, keepdims=True)
    scale = 1.0 / jnp.sqrt(pivots)
    upper = jnp.where(col_id >= row_id, done * scale, 0.0)
    inner = jnp.where(col_id < row_id, done * scale, 0.0) + jnp.where(row_id == col_id, scale, 0.0)
    l_ref[at, at] = upper.T
    row = dot(inner, w_ref[at, :])
    block_id = lax.broadcasted_iota(jnp.int32, (BLK, size), 1) // BLK
    row = jnp.where(block_id == k, jnp.concatenate([inner] * count, axis=1), row)
    x_ref[at, :] = jnp.where(block_id <= k, row, 0.0)
    inner_t = inner.T

    strip_row = lax.broadcasted_iota(jnp.int32, (STRIP, BLK), 0) // BLK
    per = STRIP // BLK

    @pl.loop((k + 1) // per, count // per)
    def _(i):
        there = window(i * STRIP, STRIP)
        below = strip_row + i * per > k
        old = w_ref[there, at]
        left = jnp.where(below, dot(old, inner_t), 0.0)
        l_ref[there, at] = jnp.where(below, left, l_ref[there, at])
        w_ref[there, at] = jnp.where(below, 0.0, old)
        w_ref[there, :] = w_ref[there, :] - dot(left, row)


def panel_kernel(
    depth, row_devices, pieces, chunks, part_ref, left_ref, u_ref, a_ref, out_ref, lcol_ref,
    w_ref, l_ref, x_ref, acc, come, got, left_own, local_sem,
    sends, recvs, pair_send, pair_recv, line_send, line_recv, out_send, out_recv,
):
    me = lax.axis_index("row")
    col = lax.axis_index("col")
    chips = row_devices // 2
    chip, core = me // 2, me % 2
    share = part_ref.shape[0]
    sub = share // depth
    pair = chip * 2 + 1 - core
    cols = [(col + d) % depth for d in range(1, depth)]
    peers = [((chip + d) % chips) * 2 + core for d in range(1, chips)]
    size = w_ref.shape[0]
    width = a_ref.shape[1]
    half = acc.shape[0] // 2
    piece = half // pieces
    count = size // BLK
    load = pltpu.make_async_copy(left_ref, left_own, local_sem)
    load.start()

    barrier = pltpu.get_barrier_semaphore()
    for other in cols:
        pl.semaphore_signal(barrier, inc=1, device_id=(me, other), device_id_type=MESH)
    for other in peers + [pair]:
        pl.semaphore_signal(barrier, inc=1, device_id=(other, col), device_id_type=MESH)
    pl.semaphore_wait(barrier, depth + chips - 1)

    def groups_of(holder):
        return ((holder + 1) * share - 1) // GROUP + 1

    def over(holder, act):
        @pl.loop(0, groups_of(holder))
        def _(g):
            act(g, window(g * GROUP, GROUP))

    mine = window(me * share + col * sub, sub)

    def first(d, g, at):
        return remote(
            part_ref.at[window(cols[d] * sub, sub), at], got.at[d, :, at], sends.at[d, g], recvs.at[d, g], (me, cols[d])
        )

    def second(d, g, at):
        n = depth - 1 + d
        ref = w_ref.at[mine, at]
        return remote(ref, ref, sends.at[n, g], recvs.at[n, g], (me, cols[d]))

    def third(d, holder, g, at):
        n = 2 * (depth - 1) + d
        ref = w_ref.at[window(holder * share, share), at]
        return remote(ref, ref, sends.at[n, g], recvs.at[n, g], (peers[d], col))

    def fourth(d, holder, g, at):
        ref = w_ref.at[window(holder * share, share), at]
        return remote(ref, ref, pair_send.at[d, g], pair_recv.at[d, g], (pair, col))

    holders = [((chip + chips - d) % chips) * 2 + core for d in range(chips)]
    others = [((chip + chips - d) % chips) * 2 + 1 - core for d in range(chips)]
    for d in range(depth - 1):
        over(me, lambda g, at: first(d, g, at).start())

    mine_cols = window(col * width, width)
    strips = half // FILL

    def fill(q):
        @pl.loop(0, 2)
        def _(way):
            at = window(way * half + q * FILL, FILL)
            acc[at, :] = -lax.dot_general(left_own[at, :], u_ref[...], TRANS, preferred_element_type=F32)
            acc[at, mine_cols] = acc[at, mine_cols] + a_ref[at, :]

    def line(way, i, target):
        at = window(way * half + i * piece, piece)
        return remote(acc.at[at, :], come.at[at, :], line_send.at[way, i], line_recv.at[way, i], (me, target))

    def pass_on(way, i, seat, target):
        @pl.when(jnp.logical_and(i >= 0, i < pieces))
        def _():
            at = window(way * half + i * piece, piece)

            @pl.when(seat > 0)
            def _():
                line(way, i, target).wait_recv()
                acc[at, :] = acc[at, :] + come[at, :]

            @pl.when(seat < depth - 1)
            def _():
                line(way, i, target).start()

    up = jnp.minimum(col + 1, depth - 1)
    down = jnp.maximum(col - 1, 0)
    seat_down = depth - 1 - col

    def line_step(tick):
        pass_on(0, tick - LAG * seat_down, seat_down, down)
        pass_on(1, tick - LAG * col, col, up)

    def line_steps(lo, hi):
        @pl.loop(lo, hi)
        def _(tick):
            line_step(tick)

    def sum_share():
        def act(g, at):
            total = part_ref[window(col * sub, sub), at]
            for d in range(depth - 1):
                first(d, g, at).wait_recv()
                total = total + got[d, :, at]
            w_ref[mine, at] = total
            for d in range(depth - 1):
                second(d, g, at).start()

        over(me, act)

    def to_peers():
        def act(g, at):
            for d in range(depth - 1):
                second(d, g, at).wait_recv()
            for d in range(chips - 1):
                third(d, me, g, at).start()
            fourth(0, me, g, at).start()

        over(me, act)

    def to_pair(d):
        def act(g, at):
            third(d - 1, holders[d], g, at).wait_recv()
            fourth(d, holders[d], g, at).start()

        over(holders[d], act)

    ticks = pieces + LAG * (depth - 1)
    load.wait()
    ready = max(6, strips)

    @pl.loop(0, ready)
    def _(tick):
        @pl.when(tick < strips)
        def _():
            fill(tick)

        @pl.when(tick == 0)
        def _():
            sum_share()

        line_step(tick)

        @pl.when(tick == 2)
        def _():
            to_peers()

        @pl.when(tick == 4)
        def _():
            for d in range(1, chips - 1):
                to_pair(d)

    to_pair(chips - 1)
    for d in range(chips):
        over(others[d], lambda g, at: fourth(d, others[d], g, at).wait_recv())
    for d in range(depth - 1):
        over(me, lambda g, at: first(d, g, at).wait_send())
        over(me, lambda g, at: second(d, g, at).wait_send())
    for d in range(chips - 1):
        over(me, lambda g, at: third(d, me, g, at).wait_send())
    for d in range(chips):
        over(holders[d], lambda g, at: fourth(d, holders[d], g, at).wait_send())

    @pl.loop(0, count)
    def _(i):
        at = window(i * BLK, BLK)
        l_ref[at, :] = jnp.zeros((BLK, size), F32)
        w_ref[at, at] = (w_ref[at, at] + w_ref[at, at].T) * 0.5

        @pl.loop(i + 1, count)
        def _(j):
            there = window(j * BLK, BLK)
            w_ref[at, there] = w_ref[there, at].T

    after = min(ticks, ready + count)

    @pl.loop(0, count)
    def _(k):
        line_steps(jnp.minimum(ready + k, after), jnp.minimum(ready + k + 1, after))
        factor_step(k, w_ref, l_ref, x_ref)

    chunk = half // chunks

    def deal(way, i, c):
        at = window(way * half + i * chunk, chunk)
        return remote(
            come.at[at, c * width:(c + 1) * width], out_ref.at[at, :],
            out_send.at[i, c], out_recv.at[way, i], (me, c),
        )

    ends = [(0, 0), (1, depth - 1)]
    at_end = jnp.logical_or(col == 0, col == depth - 1)
    own_way = jnp.where(col == 0, 0, 1)

    def reach(i):
        even = after + i * (ticks - after) // chunks
        need = i * (pieces // chunks) + LAG * (depth - 1)
        return jnp.minimum(ticks, jnp.maximum(even, jnp.where(i > 0, need, after)))

    @pl.loop(0, chunks)
    def _(i):
        line_steps(reach(i), reach(i + 1))

        @pl.when(at_end)
        def _():
            at = window(own_way * half + i * chunk, chunk)
            for c in reversed(range(depth)):
                upto = (c + 1) * width
                value = dot(acc[at, :upto], x_ref[c * width:upto, :upto], ((1,), (1,)))

                @pl.when(col == c)
                def _():
                    out_ref[at, :] = value

                @pl.when(col != c)
                def _():
                    come[at, c * width:upto] = value
                    deal(own_way, i, c).start()

    lcol_ref[...] = l_ref[:, mine_cols]

    for way, end in ends:

        @pl.when(col != end)
        def _():
            @pl.loop(0, chunks)
            def _(i):
                deal(way, i, 0).wait_recv()

    @pl.when(at_end)
    def _():
        @pl.loop(0, chunks)
        def _(i):
            for c in range(depth):

                @pl.when(col != c)
                def _():
                    deal(own_way, i, c).wait_send()

    @pl.when(col > 0)
    def _():
        @pl.loop(0, pieces)
        def _(i):
            line(0, i, down).wait_send()

    @pl.when(col < depth - 1)
    def _():
        @pl.loop(0, pieces)
        def _(i):
            line(1, i, up).wait_send()


def panel(mesh, part, left, pivot_u, tiles):
    row_devices, depth = mesh.shape["row"], mesh.shape["col"]
    chips = row_devices // 2
    share, size = part.shape
    rows, width = tiles.shape
    pieces = rows // 2 // 64
    chunks = rows // 2 // 128
    links = 2 * (depth - 1) + chips - 1
    return pl.pallas_call(
        functools.partial(panel_kernel, depth, row_devices, pieces, chunks),
        out_shape=(
            jax.ShapeDtypeStruct((rows, width), F32),
            jax.ShapeDtypeStruct((size, width), F32),
        ),
        in_specs=[VM, ANY, VM, VM],
        out_specs=(VM, VM),
        scratch_shapes=[
            pltpu.VMEM((size, size), F32),
            pltpu.VMEM((size, size), F32),
            pltpu.VMEM((size, size), F32),
            pltpu.VMEM((rows, size), F32),
            pltpu.VMEM((rows, size), F32),
            pltpu.VMEM((depth - 1, share // depth, size), F32),
            pltpu.VMEM(left.shape, BF16),
            pltpu.SemaphoreType.DMA,
            pltpu.SemaphoreType.DMA((links, size // GROUP)),
            pltpu.SemaphoreType.DMA((links, size // GROUP)),
            pltpu.SemaphoreType.DMA((chips, size // GROUP)),
            pltpu.SemaphoreType.DMA((chips, size // GROUP)),
            pltpu.SemaphoreType.DMA((2, pieces)),
            pltpu.SemaphoreType.DMA((2, pieces)),
            pltpu.SemaphoreType.DMA((chunks, depth)),
            pltpu.SemaphoreType.DMA((2, chunks)),
        ],
        compiler_params=pltpu.CompilerParams(
            collective_id=0, has_side_effects=True, vmem_limit_bytes=58 * 1024 * 1024
        ),
        cost_estimate=pl.CostEstimate(flops=60_000_000_000, bytes_accessed=30_000_000, transcendentals=0),
        name="panel",
    )(part, left, pivot_u, tiles)


def local(mesh, panel_tiles, left_u, earlier_right_factors, tile_global_index):
    row_devices = mesh.shape["row"]
    tile_count = tile_global_index.shape[0]
    slots = panel_tiles.shape[0] // TILE
    here = tile_global_index == 0
    position = jnp.arange(tile_count, dtype=jnp.int32)
    owner_row = jnp.sum(jnp.where(here, position // slots, 0))
    mask = jnp.logical_and(here[None, :], (position % slots)[None, :] == jnp.arange(slots)[:, None])
    mask = jnp.sum(mask.astype(F32), axis=1)
    local_slot = jnp.sum(jnp.where(here, position % slots, 0))
    mask = jnp.broadcast_to(mask[:, None], (slots, left_u.shape[1]))
    branches = [functools.partial(spread, mesh, owner) for owner in range(row_devices)]
    left, pivot_u, part = lax.switch(
        owner_row, branches, mask, earlier_right_factors, left_u, panel_tiles,
    )
    solved, chol = panel(mesh, part, left, pivot_u, panel_tiles)
    chosen = jnp.logical_and(lax.axis_index("row") == owner_row, jnp.arange(slots) == local_slot)
    solved = solved.reshape(slots, TILE, -1)
    return jnp.where(chosen[:, None, None], chol[None], solved).reshape(panel_tiles.shape)


def solution(mesh):
    in_specs = (P("row", "col"), P("row", "col"), P("row", "col"), P())
    return jax.shard_map(
        functools.partial(local, mesh), mesh=mesh, in_specs=in_specs, out_specs=P("row", "col"), check_vma=False
    )
```

profile of v0, /device:TPU:0, one launch (start us, length us, event | category | flops | bytes accessed | tf_op | source)
XLA Modules:
  0.0 285.9 jit_solution(4295434168430127579)
XLA Ops:
  0.0 1.3 select_reduce_fusion
  1.9 0.7 broadcast_compare_fusion
  2.5 0.1 fusion
  2.6 0.1 broadcast_in_dim.39
  2.7 68.3 %conditional.1 = ((bf16[2048,1536]{1,0:T(8,128)(2,1)}, bf16[1024,1536]{1,0:T(8,128)(2,1)S(1)}, f32[128,1024]{1,0:T(8,128)})) conditional(s32[]{:T(128)} %clamp.3, (f32[2,1536]{1,0:T(2,128)S(1)}, bf16[2048,1536]{1,0:T(8,128)(2,1)}, bf16[2048,1536]{1,0:T(8,128)(2,1)}, f32[2048,256]{1,0:T(8,128)}) %tuple.29, ...), branch_computations={%region_3.4_spmd, %region_4.5_spmd, %region_5.6_spmd, %region_6.7_... | conditional | flops 20000000000 | bytes 30000008 | solution.py:678
  2.7 68.1 %spread.13 = (bf16[2048,1536]{1,0:T(8,128)(2,1)}, bf16[1024,1536]{1,0:T(8,128)(2,1)S(1)}, f32[128,1024]{1,0:T(8,128)}) custom-call(f32[2,1536]{1,0:T(2,128)S(1)} %get-tuple-element.89.mask_ref, bf16[2048,1536]{1,0:T(8,128)(2,1)} %get-tuple-element.90.v_ref, bf16[2048,1536]{1,0:T(8,128)(2,1)} %get-tuple-element.91.u_ref, f32[2048,256]{1,0:T(8,128)} %get-tuple-element.92.a_ref), custom_call_target="tpu_custom_call" | custom-call | flops 20000000000 | bytes 30000000 | tf_op jit(solution)/shard_map/cond/branch_5_fun/spread/pallas_call | solution.py:261
  71.0 210.0 %panel.1 = (f32[2048,256]{1,0:T(8,128)}, f32[1024,256]{1,0:T(8,128)}) custom-call(f32[128,1024]{1,0:T(8,128)} %get-tuple-element.106.part_ref, bf16[2048,1536]{1,0:T(8,128)(2,1)} %get-tuple-element.107.left_ref, bf16[1024,1536]{1,0:T(8,128)(2,1)S(1)} %get-tuple-element.108.u_ref, f32[2048,256]{1,0:T(8,128)} %a_ref.1), custom_call_target="tpu_custom_call" | custom-call | flops 60000002048 | bytes 30000000 | tf_op jit(solution)/shard_map/panel/pallas_call | solution.py:632
  281.6 0.7 compare_and_fusion
  282.2 0.1 broadcast_in_dim.36
  282.3 3.5 %bitcast_select_fusion = f32[2048,256]{1,0:T(8,128)} fusion(f32[2048,256]{1,0:T(8,128)} %get-tuple-element.110, f32[1024,256]{1,0:T(8,128)} %get-tuple-element.109, pred[2048]{0:T(1024)(128)(4,1)S(1)} %broadcast_in_dim.37), kind=kLoop, calls=%fused_computation | loop fusion | flops 524288 | bytes 5244928 | tf_op jit(solution)/shard_map/jit(_where)/select_n | solution.py:684
  (2 shorter events, 0.0 us)
where the time goes:
time: 285 us; the launch traced here: 286 us
  Pallas kernels  278 us (98%)
  other arithmetic  6.25 us (2%)
    pallas_call x1, Pallas kernels, panel(): pl.pallas_call(functools.partial(panel_kernel, depth, row_devices, pieces...  210 us
    pallas_call x1, Pallas kernels, spread(): pl.pallas_call(functools.partial(spread_kernel, owner, row_devices, piece...  68.1 us

commit v1 on v0

--- a/solution.py
+++ b/solution.py
@@ -572,21 +572,19 @@
     def _(i):
         line_steps(reach(i), reach(i + 1))
 
-        @pl.when(at_end)
-        def _():
-            at = window(own_way * half + i * chunk, chunk)
-            for c in reversed(range(depth)):
-                upto = (c + 1) * width
-                value = dot(acc[at, :upto], x_ref[c * width:upto, :upto], ((1,), (1,)))
-
-                @pl.when(col == c)
-                def _():
-                    out_ref[at, :] = value
-
-                @pl.when(col != c)
-                def _():
-                    come[at, c * width:upto] = value
-                    deal(own_way, i, c).start()
+        for way, end in ends:
+
+            @pl.when(col == end)
+            def _():
+                at = window(way * half + i * chunk, chunk)
+                for c in sorted(range(depth), key=lambda c: -abs(c - end)):
+                    upto = (c + 1) * width
+                    value = dot(acc[at, :upto], x_ref[c * width:upto, :upto], ((1,), (1,)))
+                    if c == end:
+                        out_ref[at, :] = value
+                    else:
+                        come[at, c * width:upto] = value
+                        deal(way, i, c).start()
 
     lcol_ref[...] = l_ref[:, mine_cols]
 

time: 285 us -> 283 us (level)
    pallas_call x1, Pallas kernels: 68.1 us -> 64.1 us  [spread(): pl.pallas_call(functools.partial(spread_kernel, owner, row_devices, piece...]
where the time goes in v1:
time: 283 us; the launch traced here: 284 us
  Pallas kernels  276 us (98%)
  other arithmetic  6.25 us (2%)
    pallas_call x1, Pallas kernels, panel(): pl.pallas_call(functools.partial(panel_kernel, depth, row_devices, pieces...  212 us
    pallas_call x1, Pallas kernels, spread(): pl.pallas_call(functools.partial(spread_kernel, owner, row_devices, piece...  64.1 us

profile of v1, /device:TPU:0, one launch (start us, length us, event | category | flops | bytes accessed | tf_op | source)
XLA Modules:
  0.0 283.6 jit_solution(2271547606107366492)
XLA Ops:
  0.0 1.3 select_reduce_fusion
  1.9 0.7 broadcast_compare_fusion
  2.5 0.1 fusion
  2.6 0.1 broadcast_in_dim.39
  2.7 64.3 %conditional.1 = ((bf16[2048,1536]{1,0:T(8,128)(2,1)}, bf16[1024,1536]{1,0:T(8,128)(2,1)S(1)}, f32[128,1024]{1,0:T(8,128)})) conditional(s32[]{:T(128)} %clamp.3, (f32[2,1536]{1,0:T(2,128)S(1)}, bf16[2048,1536]{1,0:T(8,128)(2,1)}, bf16[2048,1536]{1,0:T(8,128)(2,1)}, f32[2048,256]{1,0:T(8,128)}) %tuple.29, ...), branch_computations={%region_3.4_spmd, %region_4.5_spmd, %region_5.6_spmd, %region_6.7_... | conditional | flops 20000000000 | bytes 30000008 | solution.py:676
  2.7 64.1 %spread.15 = (bf16[2048,1536]{1,0:T(8,128)(2,1)}, bf16[1024,1536]{1,0:T(8,128)(2,1)S(1)}, f32[128,1024]{1,0:T(8,128)}) custom-call(f32[2,1536]{1,0:T(2,128)S(1)} %get-tuple-element.97.mask_ref, bf16[2048,1536]{1,0:T(8,128)(2,1)} %get-tuple-element.98.v_ref, bf16[2048,1536]{1,0:T(8,128)(2,1)} %get-tuple-element.99.u_ref, f32[2048,256]{1,0:T(8,128)} %get-tuple-element.100.a_ref), custom_call_target="tpu_custom_call" | custom-call | flops 20000000000 | bytes 30000000 | tf_op jit(solution)/shard_map/cond/branch_7_fun/spread/pallas_call | solution.py:261
  67.0 211.8 %panel.1 = (f32[2048,256]{1,0:T(8,128)}, f32[1024,256]{1,0:T(8,128)}) custom-call(f32[128,1024]{1,0:T(8,128)} %get-tuple-element.106.part_ref, bf16[2048,1536]{1,0:T(8,128)(2,1)} %get-tuple-element.107.left_ref, bf16[1024,1536]{1,0:T(8,128)(2,1)S(1)} %get-tuple-element.108.u_ref, f32[2048,256]{1,0:T(8,128)} %a_ref.1), custom_call_target="tpu_custom_call" | custom-call | flops 60000002048 | bytes 30000000 | tf_op jit(solution)/shard_map/panel/pallas_call | solution.py:630
  279.3 0.7 compare_and_fusion
  280.0 0.1 broadcast_in_dim.36
  280.1 3.5 %bitcast_select_fusion = f32[2048,256]{1,0:T(8,128)} fusion(f32[2048,256]{1,0:T(8,128)} %get-tuple-element.110, f32[1024,256]{1,0:T(8,128)} %get-tuple-element.109, pred[2048]{0:T(1024)(128)(4,1)S(1)} %broadcast_in_dim.37), kind=kLoop, calls=%fused_computation | loop fusion | flops 524288 | bytes 5244928 | tf_op jit(solution)/shard_map/jit(_where)/select_n | solution.py:682
  (2 shorter events, 0.0 us)
